TPU v7x, 512 devices: a whole 4x4x16 slice. The times are simulated.
512 devices in a mesh: dp: 8 (over x, core), expert: 64 (over z, y).
Axes of the slice: x: 4, y: 4, z: 16, core: 2. Of those that a mesh axis runs over, the one named last changes fastest.
Arguments:
- scores: int32 [64, 4096], P('expert', 'dp'), may hold values from 0 to 4095
- tokens: bfloat16 [4096, 4096], P('dp', 'expert'), may hold values from -6 to 6
- w_gate: bfloat16 [64, 1536, 4096], P('expert', 'dp'), may hold values from -0.09375 to 0.09375
- w_up: bfloat16 [64, 1536, 4096], P('expert', 'dp'), may hold values from -0.09375 to 0.09375
- w_down: bfloat16 [64, 1536, 4096], P('expert', 'dp'), may hold values from -0.15625 to 0.15625
Outputs:
- mixed: bfloat16 [4096, 4096], P('dp', 'expert')
Inputs may be any that keep to these rules, and one draw needn't show every extreme that they name: `scores`: score bins.
All inputs are finite; a program needn't handle non-finite values.
Results may differ from a plain program's by a relative error of at most 0.02.
Values may be sent and summed in bfloat16 or wider, within the bound.
A program may use at most 64 MiB of HBM per device.

v0:
```python
import jax
import jax.numpy as jnp
from jax import lax
from jax.sharding import PartitionSpec as P

CHOSEN = 4
LEVELS = 64
score_step = 1.0 / 512.0


def entering(value, axis, combine, identity):
    size, position = (lax.axis_size(axis), lax.axis_index(axis))
    everything = jax.tree.map(lambda part: lax.all_gather(part, axis), value)
    start = jax.tree.map(
        lambda part, zero: jnp.broadcast_to(jnp.asarray(zero, part.dtype), part.shape),
        value,
        identity,
    )

    def turn(k, before):
        reached = k < position
        new = combine(before, jax.tree.map(lambda part: part[k], everything))
        return jax.tree.map(lambda a, b: jnp.where(reached, a, b), new, before)

    return lax.fori_loop(0, size, turn, start)


def add_pair(earlier, later):
    return (earlier[0] + later[0], earlier[1] + later[1])


def project_rows(inputs, weight_rows):
    return lax.dot_general(
        inputs, weight_rows, (((1,), (1,)), ((), ())), preferred_element_type=jnp.float32
    )


def local(scores, tokens, w_gate, w_up, w_down):
    score_row = scores[0]
    tok_rows = score_row.shape[0]
    dp_size = lax.axis_size("dp")
    exp_size = lax.axis_size("expert")
    capacity = CHOSEN * tok_rows * dp_size // exp_size
    all_tokens = tok_rows * dp_size
    block = tokens.shape[1]
    first_tok = lax.axis_index("dp") * tok_rows
    bin_ids = jnp.arange(LEVELS, dtype=jnp.int32)
    coarse = score_row // LEVELS
    fine_bin = score_row % LEVELS
    local_coarse = jnp.sum(
        (coarse[:, None] == bin_ids[None, :]).astype(jnp.int32), axis=0, dtype=jnp.int32
    )
    coarse_counts = lax.psum(local_coarse, "dp")
    above_coarse = all_tokens - jnp.cumsum(coarse_counts, dtype=jnp.int32)
    cut_coarse = jnp.sum((above_coarse >= capacity).astype(jnp.int32), dtype=jnp.int32)
    need = capacity - jnp.sum(jnp.where(bin_ids == cut_coarse, above_coarse, 0), dtype=jnp.int32)
    inside = (coarse == cut_coarse)[:, None]
    local_fine = jnp.sum(
        ((fine_bin[:, None] == bin_ids[None, :]) & inside).astype(jnp.int32),
        axis=0,
        dtype=jnp.int32,
    )
    fine_counts = lax.psum(local_fine, "dp")
    above_fine = jnp.sum(fine_counts, dtype=jnp.int32) - jnp.cumsum(fine_counts, dtype=jnp.int32)
    cut_fine = jnp.sum((above_fine >= need).astype(jnp.int32), dtype=jnp.int32)
    allowed = need - jnp.sum(jnp.where(bin_ids == cut_fine, above_fine, 0), dtype=jnp.int32)
    cutoff = cut_coarse * LEVELS + cut_fine
    tie_mask = (score_row == cutoff).astype(jnp.int32)
    over_mask = (score_row > cutoff).astype(jnp.int32)
    tie_before, over_before = entering(
        (jnp.sum(tie_mask, dtype=jnp.int32), jnp.sum(over_mask, dtype=jnp.int32)),
        "dp",
        add_pair,
        (jnp.int32(0), jnp.int32(0)),
    )
    tie_rank = tie_before + jnp.cumsum(tie_mask, dtype=jnp.int32) - tie_mask
    chosen = (over_mask > 0) | (tie_mask > 0) & (tie_rank < allowed)
    chosen_int = chosen.astype(jnp.int32)
    slot_ids = (
        over_before
        + jnp.minimum(tie_before, allowed)
        + jnp.cumsum(chosen_int, dtype=jnp.int32)
        - chosen_int
    )
    weight = jnp.exp(score_row.astype(jnp.float32) * score_step)
    slot_dest = jnp.where(chosen, slot_ids, capacity)
    token_ids = (first_tok + jnp.arange(tok_rows, dtype=jnp.int32)).astype(jnp.float32)
    own_tables = jnp.zeros((2, capacity), jnp.float32)
    own_tables = own_tables.at[0, slot_dest].set(token_ids, mode="drop")
    own_tables = own_tables.at[1, slot_dest].set(weight, mode="drop")
    column = lax.psum(own_tables, "dp")
    table_data = lax.all_gather(column[None], "expert", axis=0, tiled=True)
    slot_tokens = table_data[:, 0, :].astype(jnp.int32)
    slot_weight = table_data[:, 1, :]
    gathered = lax.all_gather(tokens, "dp", axis=0, tiled=True)
    outgoing = gathered[slot_tokens]
    inputs = lax.all_to_all(outgoing, "expert", split_axis=0, concat_axis=2, tiled=True)[0]
    gate_val = project_rows(inputs, w_gate[0])
    up_val = project_rows(inputs, w_up[0])
    hidden = (jax.nn.silu(gate_val) * up_val).astype(jnp.bfloat16)
    computed = jnp.dot(hidden, w_down[0], preferred_element_type=jnp.float32).astype(jnp.bfloat16)[
        None
    ]
    returned = lax.all_to_all(computed, "expert", split_axis=2, concat_axis=0, tiled=True)
    term_rows = (
        jnp.zeros((all_tokens, block), jnp.float32)
        .at[slot_tokens.reshape(-1)]
        .add((returned.astype(jnp.float32) * slot_weight[:, :, None]).reshape(-1, block))
    )
    summed = lax.psum_scatter(
        term_rows.astype(jnp.bfloat16), "dp", scatter_dimension=0, tiled=True
    ).astype(jnp.float32)
    den_row = lax.psum(jnp.where(chosen, weight, jnp.float32(0.0)), "expert")
    return (summed / jnp.maximum(den_row, jnp.float32(1.0))[:, None]).astype(jnp.bfloat16)


def solution(mesh):
    in_specs = (
        P("expert", "dp"),
        P("dp", "expert"),
        P("expert", "dp", None),
        P("expert", "dp", None),
        P("expert", "dp", None),
    )
    out_specs = P("dp", "expert")
    return jax.shard_map(local, mesh=mesh, in_specs=in_specs, out_specs=out_specs, check_vma=False)
```

profile of v0, /device:TPU:8, one launch (start us, length us, event | category | flops | bytes accessed | tf_op | source)
XLA Modules:
  0.0 840.0 jit_solution(11131477647967400313)
XLA Ops:
  7.5 9.2 %psum.28 = s32[64,1]{0,1:T(1,128)S(1)} all-reduce(s32[64,1]{0,1:T(1,128)S(1)} %bitcast.111), channel_id=1, replica_groups=mesh['dp'=8,'expert'=64] {'dp'}, use_global_device_ids=true, to_apply=%region_1.2 | all-reduce | flops 64 | bytes 512 | tf_op jit(solution)/shard_map/psum | solution.py:53
  20.5 7.3 psum.29
  39.4 8.9 %all-reduce.4 = (s32[8]{0:T(128)S(1)}, s32[8]{0:T(128)S(1)}) all-reduce(s32[8]{0:T(128)S(1)} %dynamic-update-slice, s32[8]{0:T(128)S(1)} %dynamic-update-slice.1), channel_id=1, replica_groups=mesh['dp'=8,'expert'=64] {'dp'}, use_global_device_ids=true, to_apply=%add.2 | all-reduce | flops 16 | bytes 128
  48.3 20.9 %while.15 = (s32[]{:T(128)}, s32[]{:T(128)}, s32[]{:T(128)}, s32[]{:T(128)}, s32[8]{0:T(128)S(1)}, /*index=5*/s32[8]{0:T(128)S(1)}, s32[]{:T(128)}) while((s32[]{:T(128)}, s32[]{:T(128)}, s32[]{:T(128)}, s32[]{:T(128)}, s32[8]{0:T(128)S(1)}, /*index=5*/s32[8]{0:T(128)S(1)}, s32[]{:T(128)}) %tuple.38), condition=%wide.region_13.14_spmd, body=%wide.region_12.13_spmd.sunk | while | flops 7 | bytes 168 | solution.py:25
  71.8 24.8 %scatter_fusion = f32[2,256]{1,0:T(2,128)S(1)} fusion(f32[2,256]{1,0:T(2,128)S(1)} %broadcast_in_dim.38, s32[512]{0:T(512)S(1)} %bitcast.91, f32[512]{0:T(512)S(1)} %add_convert_fusion), kind=kCustom, calls=%fused_computation.1 | custom fusion | bytes 10240 | tf_op jit(solution)/shard_map/scatter | solution.py:89
  96.6 24.8 %scatter_fusion.1 = f32[2,256]{1,0:T(2,128)S(1)} fusion(f32[2,256]{1,0:T(2,128)S(1)} %scatter_fusion, s32[512]{0:T(512)S(1)} %bitcast.90, f32[512]{0:T(512)S(1)} %get-tuple-element.141), kind=kCustom, calls=%fused_computation.2 | custom fusion | bytes 10240 | tf_op jit(solution)/shard_map/scatter | solution.py:90
  121.4 12.4 %psum.30 = f32[1,2,256]{2,1,0:T(2,128)S(1)} all-reduce(f32[1,2,256]{2,1,0:T(2,128)S(1)} %bitcast.89), channel_id=1, replica_groups=mesh['dp'=8,'expert'=64] {'dp'}, use_global_device_ids=true, to_apply=%region_21.22 | all-reduce | flops 512 | bytes 4096 | tf_op jit(solution)/shard_map/psum | solution.py:91
  133.8 106.1 %all_gather.22 = f32[64,2,256]{2,1,0:T(2,128)S(1)} all-gather(f32[1,2,256]{2,1,0:T(2,128)S(1)} %psum.30), channel_id=1, replica_groups=mesh['dp'=8,'expert'=64] {'expert'}, dimensions={0}, use_global_device_ids=true | all-gather | bytes 133120 | tf_op jit(solution)/shard_map/all_gather | solution.py:92
  240.2 13.9 %all_gather.23 = bf16[4096,64]{1,0:T(8,128)(2,1)S(1)} all-gather(bf16[512,64]{1,0:T(8,128)(2,1)S(1)} %copy.44), channel_id=1, replica_groups=mesh['dp'=8,'expert'=64] {'dp'}, dimensions={0}, use_global_device_ids=true | all-gather | bytes 589824 | tf_op jit(solution)/shard_map/all_gather | solution.py:95
  254.1 57.4 %gather_fusion = bf16[16384,64]{1,0:T(8,128)(2,1)} fusion(bf16[4096,64]{1,0:T(8,128)(2,1)S(1)} %all_gather.23, s32[16384]{0:T(1024)S(1)} %broadcast_clamp_fusion), kind=kCustom, calls=%fused_computation | custom fusion | bytes 4259840 | tf_op jit(solution)/shard_map/gather | solution.py:96
  311.5 4.8 copy.45
  316.2 111.0 %all_to_all.24 = bf16[64,256,64]{1,2,0:T(8,128)(2,1)S(1)} all-to-all(bf16[64,256,64]{1,2,0:T(8,128)(2,1)} %copy.45), channel_id=1, replica_groups=mesh['dp'=8,'expert'=64] {'expert'}, dimensions={0} | all-to-all | bytes 4194304 | tf_op jit(solution)/shard_map/all_to_all | solution.py:97
  430.0 5.0 fusion
  435.0 10.0 %copy.46 = bf16[1,256,4096]{1,0,2:T(2,128)(2,1)} copy(bf16[1,256,4096]{2,1,0:T(8,128)(2,1)} %fusion) | data formatting | bytes 4194304 | tf_op jit(solution)/shard_map/broadcast_in_dim | solution.py:101
  445.6 22.9 %reduce.10 = bf16[4096,256]{1,0:T(8,128)(2,1)} reduce(bf16[4096,1,256]{2,1,0:T(2,128)(2,1)} %bitcast.95, bf16[]{:T(256)} %broadcast.348), dimensions={1}, to_apply=%bitcast.74.reduce_sub_computation | reduce | bytes 4194306
  468.5 4.0 reshape.377
  472.4 6.1 all-to-all-start.1
  478.8 99.3 %all-to-all-done.1 = bf16[64,2,8192]{2,1,0:T(2,128)(2,1)} async-done(((bf16[64,2,8192]{2,1,0:T(2,128)(2,1)}), bf16[64,2,8192]{2,1,0:T(2,128)(2,1)}, u32[]{:S(2)}, u32[]{:S(2)}) %all-to-all-start.1) | async-done | bytes 2097184 | tf_op jit(solution)/shard_map/all_to_all | solution.py:104
  578.1 10.4 %reshape.378 = bf16[4096,1,256]{2,1,0:T(2,128)(2,1)} reshape(bf16[64,2,8192]{2,1,0:T(2,128)(2,1)} %all-to-all-done.1) | data formatting | bytes 4194304
  588.6 2.5 copy.47
  594.4 6.9 copy.49
  601.2 89.1 %scatter_custom_fusion.2 = f32[4096,64]{1,0:T(8,128)} fusion(s32[16384]{0:T(1024)S(1)} %bitcast.102, f32[16384,64]{1,0:T(8,128)} %copy.49, f32[]{:T(128)} %constant.75.clone.1), kind=kCustom, calls=%fused_computation.15 | custom fusion | flops 1048576 | bytes 1049088 | tf_op jit(solution)/shard_map/scatter-add | solution.py:108
  690.3 2.7 copy.50
  693.1 138.6 %psum.31 = f32[512]{0:T(512)S(1)} all-reduce(f32[512]{0:T(512)S(1)} %get-tuple-element.131), channel_id=1, replica_groups=mesh['dp'=8,'expert'=64] {'expert'}, use_global_device_ids=true, to_apply=%region_24.25 | all-reduce | flops 512 | bytes 4096 | tf_op jit(solution)/shard_map/psum | solution.py:113
  (78 shorter events, 35.1 us)
Async XLA Ops:
  6.5 422.7 %copy-start = (bf16[1,192,4096]{2,1,0:T(8,128)(2,1)S(1)}, bf16[1,192,4096]{2,1,0:T(8,128)(2,1)}, u32[]{:S(2)}) copy-start(bf16[1,192,4096]{2,1,0:T(8,128)(2,1)} %param.11) | copy-start | bytes 4718596
  96.6 143.5 %copy-start.4 = (bf16[512,64]{0,1:T(8,128)(2,1)S(1)}, bf16[512,64]{0,1:T(8,128)(2,1)}, u32[]{:S(2)}) copy-start(bf16[512,64]{0,1:T(8,128)(2,1)} %param.8) | copy-start | bytes 196612
  316.2 112.4 %copy-start.2 = (bf16[1,192,4096]{2,1,0:T(8,128)(2,1)S(1)}, bf16[1,192,4096]{2,1,0:T(8,128)(2,1)}, u32[]{:S(2)}) copy-start(bf16[1,192,4096]{2,1,0:T(8,128)(2,1)} %param.9) | copy-start | bytes 4718596
  427.3 1.4 copy-start.1
  428.6 1.4 copy-start.3
  472.4 105.7 %all-to-all-start.1 = ((bf16[64,2,8192]{2,1,0:T(2,128)(2,1)}), bf16[64,2,8192]{2,1,0:T(2,128)(2,1)}, u32[]{:S(2)}, u32[]{:S(2)}) async-start(bf16[64,2,8192]{2,1,0:T(2,128)(2,1)} %reshape.377), calls=%async_computation.1 | async-start | bytes 4194304 | tf_op jit(solution)/shard_map/all_to_all | solution.py:104
  478.6 353.1 %reduce-scatter.2.cloned.1.call-start = ((), (), s32[]{:S(2)}) async-start(), calls=%async_computation.3 | async-start | bytes 589824 | tf_op jit(solution)/shard_map/reduce_scatter | solution.py:110
Sparse Core Ops, SparseCore 0:
  693.2 28.9 reduce-scatter.1
where the time goes:
time: 842 us; the launch traced here: 840 us
  blocking collectives  407 us (48%)
  local copies, waits for them, and re-layouts  166 us (20%)
  other arithmetic  128 us (15%)
  waiting for transfers between devices  99.3 us (12%)
  between operations  16.3 us (2%)
  loops' own time  10.4 us (1%)
    psum x1, blocking collectives, local(): den_row = lax.psum(jnp.where(chosen, weight, jnp.float32(0.0)), 'expert')  139 us
    all_to_all x1, blocking collectives, local(): lax.all_to_all(outgoing, 'expert', split_axis=0, concat_axis=2, tiled=True)  111 us
    all_gather x1, blocking collectives, local(): table_data = lax.all_gather(column[None], 'expert', axis=0, tiled=True)  106 us
    all_to_all x1, waiting for transfers between devices, local(): lax.all_to_all(computed, 'expert', split_axis=2, concat_axis=0, tiled=True)  99.3 us
    scatter-add x1, other arithmetic, local(): term_rows = jnp.zeros((all_tokens, block), jnp.float32).at[slot_tokens.re...  89.1 us
    gather x2, local copies, waits for them, and re-layouts, local(): outgoing = gathered[slot_tokens]  62.2 us
    scatter x1, local copies, waits for them, and re-layouts, local(): own_tables = own_tables.at[0, slot_dest].set(token_ids, mode='drop')  24.8 us
    scatter x1, local copies, waits for them, and re-layouts, local(): own_tables = own_tables.at[1, slot_dest].set(weight, mode='drop')  24.8 us
  transfers between devices with their start and end apart: 2, of which 1 were waited for; matrix products, arithmetic and copies ran while one was open for 0% of the time, Pallas kernels for 0%

commit v1 on v0

--- a/solution.py
+++ b/solution.py
@@ -1,11 +1,23 @@
+import functools
 import jax
 import jax.numpy as jnp
 from jax import lax
 from jax.sharding import PartitionSpec as P
+from jax.lax import all_to_all, axis_size
 
 CHOSEN = 4
 LEVELS = 64
 score_step = 1.0 / 512.0
+
+
+def advance_columns(tile_in, which_axis):
+    return jnp.concatenate(
+        all_to_all(jnp.stack([tile_in for _ in range(axis_size(which_axis))]), which_axis, 0, 0),
+        axis=0,
+    )
+
+
+cards_order = functools.partial(advance_columns, which_axis="expert")
 
 
 def entering(value, axis, combine, identity):
@@ -89,7 +101,7 @@
     own_tables = own_tables.at[0, slot_dest].set(token_ids, mode="drop")
     own_tables = own_tables.at[1, slot_dest].set(weight, mode="drop")
     column = lax.psum(own_tables, "dp")
-    table_data = lax.all_gather(column[None], "expert", axis=0, tiled=True)
+    table_data = cards_order(column[None])
     slot_tokens = table_data[:, 0, :].astype(jnp.int32)
     slot_weight = table_data[:, 1, :]
     gathered = lax.all_gather(tokens, "dp", axis=0, tiled=True)

time: 842 us -> 760 us (0.903)
  blocking collectives: 407 us -> 303 us
  starting transfers between devices: 6.18 us -> 24.9 us
    all_gather x1 -> x0, blocking collectives: 106 us -> none  [local(): table_data = lax.all_gather(column[None], 'expert', axis=0, tiled=True)]
    all_to_all x0 -> x1, starting transfers between devices: none -> 18.7 us  [advance_columns(): all_to_all(jnp.stack([tile_in for _ in range(axis_size(which_axis))]), wh...]
  transfers between devices with their start and end apart: 2 -> 3, of which waited for: 1 -> 2; matrix products, arithmetic and copies ran while one was open for 0% -> 0% of each run, Pallas kernels for 0% -> 0%
where the time goes in v1:
time: 760 us; the launch traced here: 758 us
  blocking collectives  303 us (40%)
  local copies, waits for them, and re-layouts  167 us (22%)
  other arithmetic  128 us (17%)
  waiting for transfers between devices  102 us (13%)
  starting transfers between devices  24.9 us (3%)
  between operations  16.3 us (2%)
  loops' own time  10.4 us (1%)
    psum x1, blocking collectives, local(): den_row = lax.psum(jnp.where(chosen, weight, jnp.float32(0.0)), 'expert')  139 us
    all_to_all x1, blocking collectives, local(): lax.all_to_all(outgoing, 'expert', split_axis=0, concat_axis=2, tiled=True)  113 us
    all_to_all x1, waiting for transfers between devices, local(): lax.all_to_all(computed, 'expert', split_axis=2, concat_axis=0, tiled=True)  99.3 us
    scatter-add x1, other arithmetic, local(): term_rows = jnp.zeros((all_tokens, block), jnp.float32).at[slot_tokens.re...  89.1 us
    gather x2, local copies, waits for them, and re-layouts, local(): outgoing = gathered[slot_tokens]  62.2 us
    scatter x1, local copies, waits for them, and re-layouts, local(): own_tables = own_tables.at[0, slot_dest].set(token_ids, mode='drop')  24.8 us
    scatter x1, local copies, waits for them, and re-layouts, local(): own_tables = own_tables.at[1, slot_dest].set(weight, mode='drop')  24.8 us
    unnamed x2, other arithmetic  23.5 us
  transfers between devices with their start and end apart: 3, of which 2 were waited for; matrix products, arithmetic and copies ran while one was open for 0% of the time, Pallas kernels for 0%

profile of v1, /device:TPU:8, one launch (start us, length us, event | category | flops | bytes accessed | tf_op | source)
XLA Modules:
  0.0 758.1 jit_solution(15596121218694810841)
XLA Ops:
  7.5 9.2 %psum.28 = s32[64,1]{0,1:T(1,128)S(1)} all-reduce(s32[64,1]{0,1:T(1,128)S(1)} %bitcast.112), channel_id=1, replica_groups=mesh['dp'=8,'expert'=64] {'dp'}, use_global_device_ids=true, to_apply=%region_1.2 | all-reduce | flops 64 | bytes 512 | tf_op jit(solution)/shard_map/psum | solution.py:65
  20.5 7.3 psum.29
  39.4 8.9 %all-reduce.4 = (s32[8]{0:T(128)S(1)}, s32[8]{0:T(128)S(1)}) all-reduce(s32[8]{0:T(128)S(1)} %dynamic-update-slice, s32[8]{0:T(128)S(1)} %dynamic-update-slice.1), channel_id=1, replica_groups=mesh['dp'=8,'expert'=64] {'dp'}, use_global_device_ids=true, to_apply=%add.2 | all-reduce | flops 16 | bytes 128
  48.3 20.9 %while.15 = (s32[]{:T(128)}, s32[]{:T(128)}, s32[]{:T(128)}, s32[]{:T(128)}, s32[8]{0:T(128)S(1)}, /*index=5*/s32[8]{0:T(128)S(1)}, s32[]{:T(128)}) while((s32[]{:T(128)}, s32[]{:T(128)}, s32[]{:T(128)}, s32[]{:T(128)}, s32[8]{0:T(128)S(1)}, /*index=5*/s32[8]{0:T(128)S(1)}, s32[]{:T(128)}) %tuple.38), condition=%wide.region_13.14_spmd, body=%wide.region_12.13_spmd.sunk | while | flops 7 | bytes 168 | solution.py:37
  71.8 24.8 %scatter_fusion = f32[2,256]{1,0:T(2,128)S(1)} fusion(f32[2,256]{1,0:T(2,128)S(1)} %broadcast_in_dim.20, s32[512]{0:T(512)S(1)} %bitcast.90, f32[512]{0:T(512)S(1)} %add_convert_fusion), kind=kCustom, calls=%fused_computation.1 | custom fusion | bytes 10240 | tf_op jit(solution)/shard_map/scatter | solution.py:101
  96.6 24.8 %scatter_fusion.1 = f32[2,256]{1,0:T(2,128)S(1)} fusion(f32[2,256]{1,0:T(2,128)S(1)} %scatter_fusion, s32[512]{0:T(512)S(1)} %bitcast.89, f32[512]{0:T(512)S(1)} %get-tuple-element.141), kind=kCustom, calls=%fused_computation.2 | custom fusion | bytes 10240 | tf_op jit(solution)/shard_map/scatter | solution.py:102
  121.4 12.4 %psum.30 = f32[2,256]{1,0:T(2,128)S(1)} all-reduce(f32[2,256]{1,0:T(2,128)S(1)} %scatter_fusion.1), channel_id=1, replica_groups=mesh['dp'=8,'expert'=64] {'dp'}, use_global_device_ids=true, to_apply=%region_21.22 | all-reduce | flops 512 | bytes 4096 | tf_op jit(solution)/shard_map/psum | solution.py:103
  134.5 18.7 %all-to-all-start = ((f32[64,1,2,256]{3,2,1,0:T(2,128)}), f32[64,1,2,256]{3,2,1,0:T(2,128)S(1)}, u32[]{:S(2)}, u32[]{:S(2)}) async-start(f32[64,1,2,256]{3,2,1,0:T(2,128)} %stack.3), calls=%async_computation | async-start | bytes 262144 | tf_op jit(solution)/shard_map/all_to_all | solution.py:15
  153.4 13.8 %all_gather.19 = bf16[4096,64]{1,0:T(8,128)(2,1)S(1)} all-gather(bf16[512,64]{1,0:T(8,128)(2,1)S(1)} %copy.44), channel_id=1, replica_groups=mesh['dp'=8,'expert'=64] {'dp'}, dimensions={0}, use_global_device_ids=true | all-gather | bytes 589824 | tf_op jit(solution)/shard_map/all_gather | solution.py:107
  167.2 2.6 all-to-all-done
  170.0 57.4 %gather_fusion = bf16[16384,64]{1,0:T(8,128)(2,1)} fusion(bf16[4096,64]{1,0:T(8,128)(2,1)S(1)} %all_gather.19, s32[16384]{0:T(1024)S(1)} %broadcast_clamp_fusion), kind=kCustom, calls=%fused_computation | custom fusion | bytes 4259840 | tf_op jit(solution)/shard_map/gather | solution.py:108
  227.4 4.8 copy.45
  232.2 113.2 %all_to_all.29 = bf16[64,256,64]{1,2,0:T(8,128)(2,1)S(1)} all-to-all(bf16[64,256,64]{1,2,0:T(8,128)(2,1)} %copy.45), channel_id=1, replica_groups=mesh['dp'=8,'expert'=64] {'expert'}, dimensions={0} | all-to-all | bytes 4194304 | tf_op jit(solution)/shard_map/all_to_all | solution.py:109
  348.1 5.0 fusion
  353.1 10.0 %copy.46 = bf16[1,256,4096]{1,0,2:T(2,128)(2,1)} copy(bf16[1,256,4096]{2,1,0:T(8,128)(2,1)} %fusion) | data formatting | bytes 4194304 | tf_op jit(solution)/shard_map/broadcast_in_dim | solution.py:113
  363.7 22.9 %reduce.10 = bf16[4096,256]{1,0:T(8,128)(2,1)} reduce(bf16[4096,1,256]{2,1,0:T(2,128)(2,1)} %bitcast.94, bf16[]{:T(256)} %broadcast.350), dimensions={1}, to_apply=%bitcast.74.reduce_sub_computation | reduce | bytes 4194306
  386.6 4.0 reshape.383
  390.5 6.1 all-to-all-start.2
  396.9 99.3 %all-to-all-done.2 = bf16[64,2,8192]{2,1,0:T(2,128)(2,1)} async-done(((bf16[64,2,8192]{2,1,0:T(2,128)(2,1)}), bf16[64,2,8192]{2,1,0:T(2,128)(2,1)}, u32[]{:S(2)}, u32[]{:S(2)}) %all-to-all-start.2) | async-done | bytes 2097184 | tf_op jit(solution)/shard_map/all_to_all | solution.py:116
  496.2 10.4 %reshape.384 = bf16[4096,1,256]{2,1,0:T(2,128)(2,1)} reshape(bf16[64,2,8192]{2,1,0:T(2,128)(2,1)} %all-to-all-done.2) | data formatting | bytes 4194304
  512.5 6.9 copy.49
  519.3 89.1 %scatter_custom_fusion.2 = f32[4096,64]{1,0:T(8,128)} fusion(s32[16384]{0:T(1024)S(1)} %bitcast.103, f32[16384,64]{1,0:T(8,128)} %copy.49, f32[]{:T(128)} %constant.75.clone.1), kind=kCustom, calls=%fused_computation.15 | custom fusion | flops 1048576 | bytes 1049088 | tf_op jit(solution)/shard_map/scatter-add | solution.py:120
  608.4 2.7 copy.50
  611.2 138.6 %psum.31 = f32[512]{0:T(512)S(1)} all-reduce(f32[512]{0:T(512)S(1)} %get-tuple-element.131), channel_id=1, replica_groups=mesh['dp'=8,'expert'=64] {'expert'}, use_global_device_ids=true, to_apply=%region_24.25 | all-reduce | flops 512 | bytes 4096 | tf_op jit(solution)/shard_map/psum | solution.py:125
  (80 shorter events, 38.3 us)
Async XLA Ops:
  6.5 340.8 %copy-start = (bf16[1,192,4096]{2,1,0:T(8,128)(2,1)S(1)}, bf16[1,192,4096]{2,1,0:T(8,128)(2,1)}, u32[]{:S(2)}) copy-start(bf16[1,192,4096]{2,1,0:T(8,128)(2,1)} %param.11) | copy-start | bytes 4718596
  96.6 56.6 %copy-start.4 = (bf16[512,64]{0,1:T(8,128)(2,1)S(1)}, bf16[512,64]{0,1:T(8,128)(2,1)}, u32[]{:S(2)}) copy-start(bf16[512,64]{0,1:T(8,128)(2,1)} %param.8) | copy-start | bytes 196612
  134.5 35.4 %all-to-all-start = ((f32[64,1,2,256]{3,2,1,0:T(2,128)}), f32[64,1,2,256]{3,2,1,0:T(2,128)S(1)}, u32[]{:S(2)}, u32[]{:S(2)}) async-start(f32[64,1,2,256]{3,2,1,0:T(2,128)} %stack.3), calls=%async_computation | async-start | bytes 262144 | tf_op jit(solution)/shard_map/all_to_all | solution.py:15
  232.2 114.6 %copy-start.2 = (bf16[1,192,4096]{2,1,0:T(8,128)(2,1)S(1)}, bf16[1,192,4096]{2,1,0:T(8,128)(2,1)}, u32[]{:S(2)}) copy-start(bf16[1,192,4096]{2,1,0:T(8,128)(2,1)} %param.9) | copy-start | bytes 4718596
  345.4 1.4 copy-start.1
  346.7 1.4 copy-start.3
  390.5 105.7 %all-to-all-start.2 = ((bf16[64,2,8192]{2,1,0:T(2,128)(2,1)}), bf16[64,2,8192]{2,1,0:T(2,128)(2,1)}, u32[]{:S(2)}, u32[]{:S(2)}) async-start(bf16[64,2,8192]{2,1,0:T(2,128)(2,1)} %reshape.383), calls=%async_computation.2 | async-start | bytes 4194304 | tf_op jit(solution)/shard_map/all_to_all | solution.py:116
  396.7 353.1 %reduce-scatter.2.cloned.1.call-start = ((), (), s32[]{:S(2)}) async-start(), calls=%async_computation.4 | async-start | bytes 589824 | tf_op jit(solution)/shard_map/reduce_scatter | solution.py:122
Sparse Core Ops, SparseCore 0:
  611.3 29.0 reduce-scatter.1
